TPU v7x, 32 devices: a whole 2x2x4 slice. The times are simulated.
32 devices in a mesh: samp: 4 (over x, core), snp: 4 (over z), gene: 2 (over y).
Axes of the slice: x: 2, y: 2, z: 4, core: 2. Of those that a mesh axis runs over, the one named last changes fastest.
Arguments:
- dosage: bfloat16 [18432, 1024], P(('samp', 'gene'), 'snp'), may hold values from 0 to 2
- snp_scale: float32 [1024], P('snp'), may hold values from 0.5 to 2
- covariates: float32 [18432, 64], P(('samp', 'gene'))
- previous: bfloat16 [18432, 1024], P(('samp', 'gene'), 'snp')
- expression: bfloat16 [18432, 20480], P('samp', 'gene')
Outputs:
- resid: bfloat16 [18432, 1024], P(('samp', 'gene'), 'snp')
- zscores: bfloat16 [1024, 20480], P('snp', 'gene')
All inputs are finite; a program needn't handle non-finite values.
Results may differ from a plain program's by a relative error of at most 0.001.
Values may be sent and summed in bfloat16 or wider, within the bound.
No kernel may reach another device: no remote copies, remote signals or barrier semaphores. Data moves between devices by JAX's collectives and lax.ppermute only.
A program may use at most 192 MiB of HBM per device.

v0:
```python
import jax
import jax.numpy as jnp
from jax import lax
from jax.sharding import PartitionSpec as P


def on_device(dosage, snp_scale, covariates, previous, expression):
    highest = lax.Precision.HIGHEST
    decoded = dosage.astype(jnp.float32) * snp_scale[None, :]
    gram = jnp.dot(covariates.T, covariates, precision=highest)
    cross = jnp.dot(covariates.T, decoded, precision=highest)
    gram, cross = lax.psum((gram, cross), ("samp", "gene"))
    factor = jnp.linalg.cholesky(gram)
    coef = jax.scipy.linalg.cho_solve((factor, True), cross)
    resid = (decoded - jnp.dot(covariates, coef, precision=highest)).astype(jnp.bfloat16)
    piece = lax.all_gather(previous, "gene", axis=0, tiled=True)
    partial_scores = lax.dot_general(
        piece, expression, (((0,), (0,)), ((), ())), preferred_element_type=jnp.float32
    )
    x_sq = jnp.einsum("sp,sp->p", piece, piece, preferred_element_type=jnp.float32)
    scores, x_sq = (partial_scores, x_sq)
    y_sq = jnp.einsum("sg,sg->g", expression, expression, preferred_element_type=jnp.float32)
    samples = expression.shape[0] * lax.axis_size("samp")
    root = jnp.sqrt(jnp.float32(samples))
    shares, y_share = (
        lax.psum_scatter(scores, "samp", scatter_dimension=1, tiled=True),
        lax.psum_scatter(y_sq, "samp", scatter_dimension=0, tiled=True),
    )
    x_sq = lax.psum(x_sq, "samp")
    denom = jnp.sqrt(x_sq + 1e-06)[:, None] * jnp.sqrt(y_share + 1e-06)[None, :]
    z_part = (root * shares / denom).astype(jnp.bfloat16)
    zscores = lax.all_gather(z_part, "samp", axis=1, tiled=True)
    return (resid, zscores)


def solution(mesh):
    placed = (
        P(("samp", "gene"), "snp"),
        P("snp"),
        P(("samp", "gene"), None),
        P(("samp", "gene"), "snp"),
        P("samp", "gene"),
    )
    return jax.shard_map(
        on_device,
        mesh=mesh,
        in_specs=placed,
        out_specs=(P(("samp", "gene"), "snp"), P("snp", "gene")),
        check_vma=False,
    )
```

profile of v0, /device:TPU:0, one launch (start us, length us, event | category | flops | bytes accessed | tf_op | source)
XLA Modules:
  0.0 232.6 jit_solution(6112075205556040852)
XLA Ops:
  8.0 0.0 all-gather.3.cloned.1.call-start
  8.1 0.7 all-gather.3.cloned.1.call-update
  8.7 0.0 reduce-scatter.2.cloned.1.call-start
  8.8 40.4 %all-gather.3.cloned.1.call-done = bf16[4608,256]{1,0:T(8,128)(2,1)} async-done(((bf16[2304,256]{1,0:T(8,128)(2,1)}), bf16[4608,256]{1,0:T(8,128)(2,1)}) %all-gather.3.cloned.1.call-update) | async-done | bytes 2359312 | tf_op jit(solution)/shard_map/all_gather | solution.py:16
  49.2 39.2 %fusion.15 = f32[256,10240]{1,0:T(8,128)} fusion(bf16[4608,256]{1,0:T(8,128)(2,1)} %all-gather.3.cloned.1.call-done, bf16[4608,10240]{1,0:T(8,128)(2,1)} %param.9), kind=kOutput, calls=%fused_computation.28 | convolution fusion | flops 24159191040 | bytes 107216896 | tf_op jit(solution)/shard_map/dot_general | solution.py:17
  88.4 0.0 reduce-scatter.2.cloned.1.call-update
  88.4 0.0 all-reduce.4.cloned.1.call-start
  88.5 1.2 copy-done.1
  89.6 0.7 copy.11
  90.4 2.7 %fusion.6 = f32[64,256]{0,1:T(8,128)} fusion(f32[2304,64]{0,1:T(8,128)S(1)} %copy-done, bf16[2304,256]{0,1:T(8,128)(2,1)S(1)} %copy.11, f32[256]{0:T(256)S(1)} %copy-done.2), kind=kOutput, calls=%fused_computation.11 | convolution fusion | flops 454164480 | bytes 1836032 | tf_op jit(solution)/shard_map/dot_general | solution.py:11
  93.1 0.0 all-reduce.4.cloned.1.call-update
  93.1 0.0 all-gather.5.cloned.1.call-start
  93.2 35.1 %fusion = f32[10240]{0:T(1024)S(1)} fusion(bf16[4608,10240]{1,0:T(8,128)(2,1)} %param.9), kind=kLoop, calls=%fused_computation.1 | loop fusion | flops 141547520 | bytes 94412800 | tf_op jit(solution)/shard_map/sg,sg->g/dot_general | solution.py:22
  128.3 0.6 dynamic-slice
  129.5 2.4 %fusion.1 = f32[256]{0:T(256)S(1)} fusion(bf16[4608,256]{1,0:T(8,128)(2,1)} %all-gather.3.cloned.1.call-done), kind=kLoop, calls=%fused_computation.3 | loop fusion | flops 3538688 | bytes 2360320 | tf_op jit(solution)/shard_map/sp,sp->p/dot_general | solution.py:20
  131.9 13.8 %all-reduce.1 = (f32[10240]{0:T(1024)S(1)}, f32[256]{0:T(256)S(1)}) all-reduce(f32[10240]{0:T(1024)S(1)} %fusion, f32[256]{0:T(256)S(1)} %fusion.1), channel_id=3, replica_groups=mesh['samp'=4,'snp'=4,'gene'=2] {'samp'}, use_global_device_ids=true, to_apply=%region_6.7.clone | all-reduce | flops 10496 | bytes 83968
  145.7 0.1 fusion.13
  145.8 28.1 %reduce-scatter.2.cloned.1.call-done = f32[256,2560]{1,0:T(8,128)} async-done(((f32[256,10240]{1,0:T(8,128)}), f32[256,2560]{1,0:T(8,128)}) %reduce-scatter.2.cloned.1.call-update) | async-done | bytes 2621456 | tf_op jit(solution)/shard_map/reduce_scatter | solution.py:26
  173.9 3.3 %divide_convert_fusion = bf16[256,2560]{1,0:T(8,128)(2,1)} fusion(f32[256,2560]{1,0:T(8,128)} %reduce-scatter.2.cloned.1.call-done, f32[2560]{0:T(1024)S(1)} %fusion.13, f32[256]{0:T(256)S(1)} %add_sqrt_fusion), kind=kLoop, calls=%fused_computation.7 | loop fusion | flops 2621440 | bytes 3943424 | tf_op jit(solution)/shard_map/convert_element_type | solution.py:31
  177.2 0.6 fusion.14
  177.9 25.0 %psum.21 = f32[64,64]{0,1:T(8,128)S(1)} all-reduce(f32[64,64]{0,1:T(8,128)S(1)} %fusion.14), channel_id=1, replica_groups=mesh['samp'=4,'snp'=4,'gene'=2] {'samp','gene'}, use_global_device_ids=true, to_apply=%region_0.0 | all-reduce | flops 4096 | bytes 32768 | tf_op jit(solution)/shard_map/psum | solution.py:12
  202.9 0.1 copy.13
  203.0 5.8 %cholesky.16 = f32[64,64]{1,0:T(8,128)S(1)} custom-call(f32[64,64]{1,0:T(8,128)S(1)} %fusion.12), custom_call_target="Cholesky" | custom-call | tf_op jit(solution)/shard_map/jit(cholesky)/cholesky | solution.py:13
  208.9 0.7 compare_reduce_fusion
  209.5 0.6 fusion.7
  210.2 4.9 %custom-call.10 = f32[1,64,64]{1,2,0:T(8,128)S(1)} custom-call(f32[1,64,64]{2,1,0:T(8,128)S(1)} %fusion.7), custom_call_target="InvertDiagBlocksLowerTriangular" | custom-call | tf_op jit(solution)/shard_map/jit(_cho_solve)/triangular_solve | solution.py:14
  215.1 0.0 all-reduce.4.cloned.1.call-done
  215.1 1.2 fusion.10
  216.3 0.2 fusion.8
  216.5 2.1 fusion.3
  218.6 1.4 copy.14
  220.0 5.4 %copy.30 = bf16[256,10240]{1,0:T(8,128)(2,1)} copy(bf16[256,10240]{1,0:T(8,128)(2,1)} %all-gather.5.cloned.1.call-done) | data formatting | bytes 10485760
  (12 shorter events, 0.1 us)
Async XLA Ops:
  8.0 82.4 %copy-start = (f32[2304,64]{0,1:T(8,128)S(1)}, f32[2304,64]{0,1:T(8,128)}, u32[]{:S(2)}) copy-start(f32[2304,64]{0,1:T(8,128)} %param.7) | copy-start | bytes 1769476
  8.0 41.2 %all-gather.3.cloned.1.call-start = ((), (), s32[]{:S(2)}) async-start(), calls=%async_computation.2 | async-start | bytes 3538944 | tf_op jit(solution)/shard_map/all_gather | solution.py:16
  8.7 165.2 %reduce-scatter.2.cloned.1.call-start = ((), (), s32[]{:S(2)}) async-start(), calls=%async_computation.3 | async-start | bytes 13107200 | tf_op jit(solution)/shard_map/reduce_scatter | solution.py:26
  88.4 1.3 copy-start.1
  88.4 2.0 copy-start.2
  88.4 126.7 %all-reduce.4.cloned.1.call-start = ((), (), s32[]{:S(2)}) async-start(), calls=%async_computation.1 | async-start | bytes 262144 | tf_op jit(solution)/shard_map/psum | solution.py:12
  93.1 127.0 %all-gather.5.cloned.1.call-start = ((), (), s32[]{:S(2)}) async-start(), calls=%async_computation.4 | async-start | bytes 6553600 | tf_op jit(solution)/shard_map/all_gather | solution.py:32
  93.2 35.1 %copy-start.3 = (u32[32]{0:T(128)S(1)}, u32[32]{0:T(128)}, u32[]{:S(2)}) copy-start(u32[32]{0:T(128)} %constant.58) | copy-start | bytes 388
Sparse Core Ops, SparseCore 0:
  10.4 38.7 all-gather.2
  88.5 85.3 reduce-scatter.1
  177.4 40.6 all-gather.4
Sparse Core Ops, SparseCore 1:
  93.2 121.3 all-reduce.3
where the time goes:
time: 233 us
  waiting for transfers between devices  69.2 us (30%)
  other arithmetic  53 us (23%)
  matrix products  46 us (20%)
  blocking collectives  38.8 us (17%)
  between operations  16 us (7%)
  local copies, waits for them, and re-layouts  9.4 us (4%)
    all_gather x1, waiting for transfers between devices, on_device(): piece = lax.all_gather(previous, 'gene', axis=0, tiled=True)  40.4 us
    dot_general x1, matrix products, on_device(): lax.dot_general(piece, expression, (((0,), (0,)), ((), ())), preferred_el...  39.2 us
    dot_general x1, other arithmetic, on_device(): jnp.einsum('sg,sg->g', expression, expression, preferred_element_type=jnp...  35.1 us
    reduce_scatter x1, waiting for transfers between devices, on_device(): lax.psum_scatter(scores, 'samp', scatter_dimension=1, tiled=True)  28.1 us
    psum x1, blocking collectives, on_device(): gram, cross = lax.psum((gram, cross), ('samp', 'gene'))  25 us
    unnamed x1, blocking collectives  13.8 us
    unnamed x12, local copies, waits for them, and re-layouts  9.32 us
    another operation x3, other arithmetic, on_device(): factor = jnp.linalg.cholesky(gram)  6.55 us
  transfers between devices with their start and end apart: 4, of which 2 were waited for; matrix products, arithmetic and copies ran while one was open for 27% of the time, Pallas kernels for 0%

commit v1 on v0

--- a/solution.py
+++ b/solution.py
@@ -9,7 +9,7 @@
     decoded = dosage.astype(jnp.float32) * snp_scale[None, :]
     gram = jnp.dot(covariates.T, covariates, precision=highest)
     cross = jnp.dot(covariates.T, decoded, precision=highest)
-    gram, cross = lax.psum((gram, cross), ("samp", "gene"))
+    gram, cross = lax.psum(lax.psum((gram, cross), "gene"), "samp")
     factor = jnp.linalg.cholesky(gram)
     coef = jax.scipy.linalg.cho_solve((factor, True), cross)
     resid = (decoded - jnp.dot(covariates, coef, precision=highest)).astype(jnp.bfloat16)

time: 233 us -> 262 us (1.12)
  waiting for transfers between devices: 69.2 us -> 119 us
  blocking collectives: 38.8 us -> 21.8 us
    all_gather x1, waiting for transfers between devices: 0.01 us -> 37.5 us  [on_device(): zscores = lax.all_gather(z_part, 'samp', axis=1, tiled=True)]
    psum x1 -> x2, waiting for transfers between devices: 0.03 us -> 18.7 us  [on_device(): gram, cross = lax.psum(lax.psum((gram, cross), 'gene'), 'samp')]
    unnamed x1 -> x0, blocking collectives: 13.8 us -> none
    all_gather x1, waiting for transfers between devices: 40.4 us -> 36 us  [on_device(): piece = lax.all_gather(previous, 'gene', axis=0, tiled=True)]
    psum x1 -> x2, blocking collectives: 25 us -> 21.8 us  [on_device(): gram, cross = lax.psum(lax.psum((gram, cross), 'gene'), 'samp')]
    unnamed x12 -> x10, local copies, waits for them, and re-layouts: 9.32 us -> 9.56 us
  transfers between devices with their start and end apart: 4 -> 5, of which waited for: 2 -> 4; matrix products, arithmetic and copies ran while one was open for 27% -> 38% of each run, Pallas kernels for 0% -> 0%
where the time goes in v1:
time: 262 us
  waiting for transfers between devices  119 us (45%)
  other arithmetic  51 us (19%)
  matrix products  46.1 us (18%)
  blocking collectives  21.8 us (8%)
  between operations  14.6 us (6%)
  local copies, waits for them, and re-layouts  9.63 us (4%)
    dot_general x1, matrix products, on_device(): lax.dot_general(piece, expression, (((0,), (0,)), ((), ())), preferred_el...  39.3 us
    all_gather x1, waiting for transfers between devices, on_device(): zscores = lax.all_gather(z_part, 'samp', axis=1, tiled=True)  37.5 us
    all_gather x1, waiting for transfers between devices, on_device(): piece = lax.all_gather(previous, 'gene', axis=0, tiled=True)  36 us
    dot_general x1, other arithmetic, on_device(): jnp.einsum('sg,sg->g', expression, expression, preferred_element_type=jnp...  33.1 us
    reduce_scatter x1, waiting for transfers between devices, on_device(): lax.psum_scatter(scores, 'samp', scatter_dimension=1, tiled=True)  25.8 us
    psum x2, blocking collectives, on_device(): gram, cross = lax.psum(lax.psum((gram, cross), 'gene'), 'samp')  21.8 us
    psum x2, waiting for transfers between devices, on_device(): gram, cross = lax.psum(lax.psum((gram, cross), 'gene'), 'samp')  18.7 us
    unnamed x10, local copies, waits for them, and re-layouts  9.56 us
  transfers between devices with their start and end apart: 5, of which 4 were waited for; matrix products, arithmetic and copies ran while one was open for 38% of the time, Pallas kernels for 0%

profile of v1, /device:TPU:0, one launch (start us, length us, event | category | flops | bytes accessed | tf_op | source)
XLA Modules:
  0.0 261.9 jit_solution(14941296889410369891)
XLA Ops:
  7.2 0.0 all-gather.3.cloned.1.call-start
  7.2 0.7 all-gather.3.cloned.1.call-update
  7.9 0.0 all-reduce.5.cloned.1.call-start
  8.0 1.6 copy.11
  9.6 2.7 %fusion.6 = f32[64,256]{0,1:T(8,128)} fusion(f32[2304,64]{0,1:T(8,128)S(1)} %copy-done, bf16[2304,256]{0,1:T(8,128)(2,1)S(1)} %copy.11, f32[256]{0:T(256)S(1)} %copy-done.1), kind=kOutput, calls=%fused_computation.11 | convolution fusion | flops 454164480 | bytes 1836032 | tf_op jit(solution)/shard_map/dot_general | solution.py:11
  12.3 0.0 reduce-scatter.2.cloned.1.call-start
  12.3 36.0 %all-gather.3.cloned.1.call-done = bf16[4608,256]{1,0:T(8,128)(2,1)} async-done(((bf16[2304,256]{1,0:T(8,128)(2,1)}), bf16[4608,256]{1,0:T(8,128)(2,1)}) %all-gather.3.cloned.1.call-update) | async-done | bytes 2359312 | tf_op jit(solution)/shard_map/all_gather | solution.py:16
  48.3 39.3 %fusion.15 = f32[256,10240]{1,0:T(8,128)} fusion(bf16[4608,256]{1,0:T(8,128)(2,1)} %all-gather.3.cloned.1.call-done, bf16[4608,10240]{1,0:T(8,128)(2,1)} %param.9), kind=kOutput, calls=%fused_computation.28 | convolution fusion | flops 24159191040 | bytes 107216896 | tf_op jit(solution)/shard_map/dot_general | solution.py:17
  87.7 0.0 all-reduce.7.cloned.1.call-start
  87.7 0.6 copy-done.2
  88.3 0.6 dynamic-slice
  89.5 0.6 fusion.14
  90.1 7.2 %psum.35 = f32[64,64]{0,1:T(8,128)S(1)} all-reduce(f32[64,64]{0,1:T(8,128)S(1)} %fusion.14), channel_id=1, replica_groups=mesh['samp'=4,'snp'=4,'gene'=2] {'gene'}, use_global_device_ids=true, to_apply=%region_0.0 | all-reduce | flops 4096 | bytes 32768 | tf_op jit(solution)/shard_map/psum | solution.py:12
  97.3 33.1 %fusion = f32[10240]{0:T(1024)S(1)} fusion(bf16[4608,10240]{1,0:T(8,128)(2,1)} %param.9), kind=kLoop, calls=%fused_computation.1 | loop fusion | flops 141547520 | bytes 94412800 | tf_op jit(solution)/shard_map/sg,sg->g/dot_general | solution.py:22
  130.5 0.0 all-gather.5.cloned.1.call-start
  130.6 2.4 fusion.1
  132.9 14.6 %all-reduce.1 = (f32[64,64]{0,1:T(8,128)S(1)}, f32[10240]{0:T(1024)S(1)}, f32[256]{0:T(256)S(1)}) all-reduce(f32[64,64]{0,1:T(8,128)S(1)} %psum.35, f32[10240]{0:T(1024)S(1)} %fusion, f32[256]{0:T(256)S(1)} %fusion.1), channel_id=1, replica_groups=mesh['samp'=4,'snp'=4,'gene'=2] {'samp'}, use_global_device_ids=true, to_apply=%region_1.0 | all-reduce | flops 14592 | bytes 116736 | tf_op jit(solution)/shard_map/psum | solution.py:12
  147.5 0.1 fusion.13
  147.6 25.8 %reduce-scatter.2.cloned.1.call-done = f32[256,2560]{1,0:T(8,128)} async-done(((f32[256,10240]{1,0:T(8,128)}), f32[256,2560]{1,0:T(8,128)}) %reduce-scatter.2.cloned.1.call-update) | async-done | bytes 2621456 | tf_op jit(solution)/shard_map/reduce_scatter | solution.py:26
  173.4 3.3 %divide_convert_fusion = bf16[256,2560]{1,0:T(8,128)(2,1)} fusion(f32[256,2560]{1,0:T(8,128)} %reduce-scatter.2.cloned.1.call-done, f32[2560]{0:T(1024)S(1)} %fusion.13, f32[256]{0:T(256)S(1)} %add_sqrt_fusion), kind=kLoop, calls=%fused_computation.7 | loop fusion | flops 2621440 | bytes 3943424 | tf_op jit(solution)/shard_map/convert_element_type | solution.py:31
  176.8 0.1 copy.13
  176.9 5.8 %cholesky.16 = f32[64,64]{1,0:T(8,128)S(1)} custom-call(f32[64,64]{1,0:T(8,128)S(1)} %fusion.12), custom_call_target="Cholesky" | custom-call | tf_op jit(solution)/shard_map/jit(cholesky)/cholesky | solution.py:13
  182.7 0.6 compare_reduce_fusion
  183.4 0.7 fusion.7
  184.1 4.9 %custom-call.10 = f32[1,64,64]{1,2,0:T(8,128)S(1)} custom-call(f32[1,64,64]{2,1,0:T(8,128)S(1)} %fusion.7), custom_call_target="InvertDiagBlocksLowerTriangular" | custom-call | tf_op jit(solution)/shard_map/jit(_cho_solve)/triangular_solve | solution.py:14
  188.9 18.6 %all-reduce.7.cloned.1.call-done = f32[64,256]{0,1:T(8,128)} async-done(((f32[64,256]{0,1:T(8,128)}), f32[64,256]{0,1:T(8,128)}) %all-reduce.7.cloned.1.call-update) | async-done | bytes 65552 | tf_op jit(solution)/shard_map/psum | solution.py:12
  207.6 1.2 fusion.10
  208.8 0.2 fusion.8
  209.0 2.1 fusion.3
  211.1 1.4 copy.14
  212.5 37.5 %all-gather.5.cloned.1.call-done = bf16[256,10240]{1,0:T(8,128)(2,1)} async-done(((bf16[256,2560]{1,0:T(8,128)(2,1)}), bf16[256,10240]{1,0:T(8,128)(2,1)}) %all-gather.5.cloned.1.call-update) | async-done | bytes 5242896 | tf_op jit(solution)/shard_map/all_gather | solution.py:32
  250.0 5.4 %copy.31 = bf16[256,10240]{1,0:T(8,128)(2,1)} copy(bf16[256,10240]{1,0:T(8,128)(2,1)} %all-gather.5.cloned.1.call-done) | data formatting | bytes 10485760
  (13 shorter events, 0.1 us)
Async XLA Ops:
  7.2 2.4 copy-start
  7.2 2.4 copy-start.1
  7.2 41.2 %all-gather.3.cloned.1.call-start = ((), (), s32[]{:S(2)}) async-start(), calls=%async_computation.3 | async-start | bytes 3538944 | tf_op jit(solution)/shard_map/all_gather | solution.py:16
  7.9 122.6 %all-reduce.5.cloned.1.call-start = ((), (), s32[]{:S(2)}) async-start(), calls=%async_computation.1 | async-start | bytes 262144 | tf_op jit(solution)/shard_map/psum | solution.py:12
  12.3 161.2 %reduce-scatter.2.cloned.1.call-start = ((), (), s32[]{:S(2)}) async-start(), calls=%async_computation.4 | async-start | bytes 13107200 | tf_op jit(solution)/shard_map/reduce_scatter | solution.py:26
  87.6 0.7 copy-start.2
  87.7 119.9 %all-reduce.7.cloned.1.call-start = ((), (), s32[]{:S(2)}) async-start(), calls=%async_computation.2 | async-start | bytes 262144 | tf_op jit(solution)/shard_map/psum | solution.py:12
  130.5 119.5 %all-gather.5.cloned.1.call-start = ((), (), s32[]{:S(2)}) async-start(), calls=%async_computation.5 | async-start | bytes 6553600 | tf_op jit(solution)/shard_map/all_gather | solution.py:32
Sparse Core Ops, SparseCore 0:
  9.5 38.7 all-gather.2
  51.2 21.5 all-reduce.4
  87.8 85.6 reduce-scatter.1
  175.6 31.9 all-reduce.6
  209.6 40.3 all-gather.4
